TPU v7x, 512 devices: a whole 4x4x16 slice. The times are simulated.
512 devices in a mesh: row: 16 (over y, x), col: 32 (over z, core).
Axes of the slice: x: 4, y: 4, z: 16, core: 2. Of those that a mesh axis runs over, the one named last changes fastest.
Arguments:
- momentum: float32 [4096, 14336], P('row', 'col'), may hold values from -6 to 6
- grads: bfloat16 [1, 4096, 14336], P(None, 'row', 'col'), may hold values from -6 to 6
- right_factor: float32 [128, 14336], P(None, 'col'), may hold values from -0.046875 to 0.046875
Outputs:
- new_momentum: float32 [4096, 14336], P('row', 'col')
- new_factor: float32 [128, 14336], P(None, 'col')
- update: float32 [4096, 14336], P('row', 'col')
All inputs are finite; a program needn't handle non-finite values.
Results may differ from a plain program's by a relative error of at most 0.0005.
Values sent between devices are 32-bit elements; how exact they have to be, the bound alone decides.
A program may use at most 64 MiB of HBM per device.

v0:
```python
import jax
import jax.numpy as jnp
from jax import lax
from jax.sharding import PartitionSpec as P

M = 4096
N = 14336
RANK = 128
POWER = 2
DECAY_LEFT = 0.05
EPSILON = 1e-06


def contract(first, second, first_dim, second_dim):
    return lax.dot_general(
        first,
        second,
        (((first_dim,), (second_dim,)), ((), ())),
        precision=lax.Precision.HIGHEST,
        preferred_element_type=jnp.float32,
    )


def orthonormal(gram_matrix, left_t):
    lower_f = jnp.linalg.cholesky(gram_matrix)
    return lax.linalg.triangular_solve(lower_f, left_t, left_side=True, lower=True)


def local(momentum, grads, right_factor):
    factor_t = right_factor
    moment = momentum
    blend = moment + grads[0].astype(jnp.float32)
    for sweep_index in range(POWER):
        partial_value = contract(factor_t, blend, 1, 1)
        left_t = lax.psum(partial_value, "col")
        gram_matrix = lax.psum(contract(left_t, left_t, 1, 1), "row")
        left_t = orthonormal(gram_matrix, left_t)
        right_t = lax.psum(contract(left_t, blend, 1, 0), "row")
        squares = lax.psum(jnp.sum(right_t * right_t, axis=1, keepdims=True), "col")
        factor_t = right_t / (jnp.sqrt(squares) + EPSILON)
    moment = blend - DECAY_LEFT * contract(left_t, right_t, 0, 0)
    accum = contract(left_t, factor_t, 0, 0)
    return (moment, factor_t, accum * jnp.float32((M * N / RANK) ** 0.5))


def solution(mesh):
    return jax.shard_map(
        local,
        mesh=mesh,
        in_specs=(P("row", "col"), P(None, "row", "col"), P(None, "col")),
        out_specs=(P("row", "col"), P(None, "col"), P("row", "col")),
        check_vma=False,
    )
```

profile of v0, /device:TPU:1, one launch (start us, length us, event | category | flops | bytes accessed | tf_op | source)
XLA Modules:
  0.0 1026.8 jit_solution(11263512012418945397)
XLA Ops:
  8.1 2.7 convolution_bitcast_fusion
  10.9 204.7 %all-reduce.7.cloned.1.call-done = f32[128,256]{0,1:T(8,128)} async-done(((f32[128,256]{0,1:T(8,128)}), f32[128,256]{0,1:T(8,128)}) %all-reduce.7.cloned.1.call-update) | async-done | bytes 131088 | tf_op jit(solution)/shard_map/psum | solution.py:35
  215.6 2.0 fusion.16
  217.7 108.6 %all-reduce.9.cloned.1.call-done = f32[128,128]{0,1:T(8,128)} async-done(((f32[128,128]{0,1:T(8,128)}), f32[128,128]{0,1:T(8,128)}) %all-reduce.9.cloned.1.call-update) | async-done | bytes 65552 | tf_op jit(solution)/shard_map/psum | solution.py:36
  326.3 0.9 copy.7
  328.1 11.7 %cholesky.44 = f32[128,128]{1,0:T(8,128)S(1)} custom-call(f32[128,128]{1,0:T(8,128)S(1)} %fusion.11), custom_call_target="Cholesky" | custom-call | tf_op jit(solution)/shard_map/jit(cholesky)/cholesky | solution.py:25
  341.2 9.8 custom-call.6
  351.3 1.2 fusion.15
  352.6 115.1 %all-reduce.11.cloned.1.call-done = f32[128,448]{0,1:T(8,128)} async-done(((f32[128,448]{0,1:T(8,128)}), f32[128,448]{0,1:T(8,128)}) %all-reduce.11.cloned.1.call-update) | async-done | bytes 229392 | tf_op jit(solution)/shard_map/psum | solution.py:38
  467.7 1.1 multiply_reduce_fusion.1
  468.8 48.9 %psum.59 = f32[128,1]{0,1:T(1,128)S(1)} all-reduce(f32[128,1]{0,1:T(1,128)S(1)} %bitcast.48), channel_id=1, replica_groups=mesh['row'=16,'col'=32] {'col'}, use_global_device_ids=true, to_apply=%region_6.9 | all-reduce | flops 128 | bytes 1024 | tf_op jit(solution)/shard_map/psum | solution.py:39
  517.7 1.3 fusion.1
  519.1 197.1 %all-reduce.13.cloned.1.call-done = f32[128,256]{1,0:T(8,128)} async-done(((f32[128,256]{1,0:T(8,128)}), f32[128,256]{1,0:T(8,128)}) %all-reduce.13.cloned.1.call-update) | async-done | bytes 131088 | tf_op jit(solution)/shard_map/psum | solution.py:35
  716.2 1.9 fusion.17
  718.3 108.4 %all-reduce.15.cloned.1.call-done = f32[128,128]{0,1:T(8,128)} async-done(((f32[128,128]{0,1:T(8,128)}), f32[128,128]{0,1:T(8,128)}) %all-reduce.15.cloned.1.call-update) | async-done | bytes 65552 | tf_op jit(solution)/shard_map/psum | solution.py:36
  826.7 1.0 copy.9
  827.8 11.7 %cholesky.55 = f32[128,128]{1,0:T(8,128)S(1)} custom-call(f32[128,128]{1,0:T(8,128)S(1)} %fusion.8), custom_call_target="Cholesky" | custom-call | tf_op jit(solution)/shard_map/jit(cholesky)/cholesky | solution.py:25
  840.8 9.8 custom-call.7
  850.9 1.2 fusion.14
  852.2 115.1 %all-reduce.17.cloned.1.call-done = f32[128,448]{0,1:T(8,128)} async-done(((f32[128,448]{0,1:T(8,128)}), f32[128,448]{0,1:T(8,128)}) %all-reduce.17.cloned.1.call-update) | async-done | bytes 229392 | tf_op jit(solution)/shard_map/psum | solution.py:38
  967.3 1.1 multiply_reduce_fusion
  968.4 48.9 %psum.63 = f32[128,1]{0,1:T(1,128)S(1)} all-reduce(f32[128,1]{0,1:T(1,128)S(1)} %bitcast.49), channel_id=1, replica_groups=mesh['row'=16,'col'=32] {'col'}, use_global_device_ids=true, to_apply=%region_11.14 | all-reduce | flops 128 | bytes 1024 | tf_op jit(solution)/shard_map/psum | solution.py:39
  1017.4 1.3 convolution_multiply_fusion
  1018.7 1.3 fusion
  (43 shorter events, 5.7 us)
Async XLA Ops:
  7.2 0.9 copy-start
  7.2 208.4 %all-reduce.7.cloned.1.call-start = ((), (), s32[]{:S(2)}) async-start(), calls=%async_computation | async-start | bytes 262144 | tf_op jit(solution)/shard_map/psum | solution.py:35
  10.9 315.4 %all-reduce.9.cloned.1.call-start = ((), (), s32[]{:S(2)}) async-start(), calls=%async_computation.1 | async-start | bytes 131072 | tf_op jit(solution)/shard_map/psum | solution.py:36
  217.6 133.7 %copy-start.1 = (f32[256,448]{0,1:T(8,128)S(1)}, f32[256,448]{0,1:T(8,128)}, u32[]{:S(2)}) copy-start(f32[256,448]{0,1:T(8,128)} %param.6) | copy-start | bytes 1376260
  217.6 250.1 %all-reduce.11.cloned.1.call-start = ((), (), s32[]{:S(2)}) async-start(), calls=%async_computation.2 | async-start | bytes 458752 | tf_op jit(solution)/shard_map/psum | solution.py:38
  328.1 22.9 %copy-start.4 = (f32[128,256]{0,1:T(8,128)S(1)}, f32[128,256]{0,1:T(8,128)}, u32[]{:S(2)}) copy-start(f32[128,256]{0,1:T(8,128)} %all-reduce.7.cloned.1.call-done) | copy-start | bytes 393220
  340.5 10.9 %copy-start.2 = (bf16[1,256,448]{1,2,0:T(8,128)(2,1)S(1)}, bf16[1,256,448]{1,2,0:T(8,128)(2,1)}, u32[]{:S(2)}) copy-start(bf16[1,256,448]{1,2,0:T(8,128)(2,1)} %param.7) | copy-start | bytes 688132
  352.6 363.6 %all-reduce.13.cloned.1.call-start = ((), (), s32[]{:S(2)}) async-start(), calls=%async_computation.3 | async-start | bytes 262144 | tf_op jit(solution)/shard_map/psum | solution.py:35
  467.7 50.0 %copy-start.8 = (f32[128,448]{0,1:T(8,128)S(1)}, f32[128,448]{0,1:T(8,128)}, u32[]{:S(2)}) copy-start(f32[128,448]{0,1:T(8,128)} %all-reduce.11.cloned.1.call-done) | copy-start | bytes 688132
  519.0 307.7 %all-reduce.15.cloned.1.call-start = ((), (), s32[]{:S(2)}) async-start(), calls=%async_computation.4 | async-start | bytes 131072 | tf_op jit(solution)/shard_map/psum | solution.py:36
  718.1 249.3 %all-reduce.17.cloned.1.call-start = ((), (), s32[]{:S(2)}) async-start(), calls=%async_computation.5 | async-start | bytes 458752 | tf_op jit(solution)/shard_map/psum | solution.py:38
  826.7 1.0 copy-start.7
  827.7 22.9 %copy-start.5 = (f32[128,256]{1,0:T(8,128)S(1)}, f32[128,256]{1,0:T(8,128)}, u32[]{:S(2)}) copy-start(f32[128,256]{1,0:T(8,128)} %all-reduce.13.cloned.1.call-done) | copy-start | bytes 393220
  967.3 50.0 %copy-start.3 = (f32[128,448]{0,1:T(8,128)S(1)}, f32[128,448]{0,1:T(8,128)}, u32[]{:S(2)}) copy-start(f32[128,448]{0,1:T(8,128)} %all-reduce.17.cloned.1.call-done) | copy-start | bytes 688132
  1017.4 1.3 copy-start.6
Sparse Core Ops, SparseCore 0:
  11.0 204.5 all-reduce.6
  219.3 106.8 all-reduce.8
  352.7 114.9 all-reduce.10
  519.1 196.9 all-reduce.12
  719.8 106.8 all-reduce.14
  852.3 114.9 all-reduce.16
where the time goes:
time: 1030 us
  waiting for transfers between devices  849 us (82%)
  blocking collectives  97.8 us (9%)
  other arithmetic  48.8 us (5%)
  between operations  14.3 us (1%)
  matrix products  13.5 us (1%)
    psum x2, waiting for transfers between devices, local(): left_t = lax.psum(partial_value, 'col')  402 us
    psum x2, waiting for transfers between devices, local(): right_t = lax.psum(contract(left_t, blend, 1, 0), 'row')  230 us
    psum x2, waiting for transfers between devices, local(): gram_matrix = lax.psum(contract(left_t, left_t, 1, 1), 'row')  217 us
    psum x2, blocking collectives, local(): squares = lax.psum(jnp.sum(right_t * right_t, axis=1, keepdims=True), 'col')  97.8 us
    another operation x6, other arithmetic, orthonormal(): lower_f = jnp.linalg.cholesky(gram_matrix)  24.8 us
    another operation x4, other arithmetic, orthonormal(): lax.linalg.triangular_solve(lower_f, left_t, left_side=True, lower=True)  21 us
  transfers between devices with their start and end apart: 6, of which 6 were waited for; matrix products, arithmetic and copies ran while one was open for 0% of the time, Pallas kernels for 0%

commit v1 on v0

--- a/solution.py
+++ b/solution.py
@@ -36,7 +36,9 @@
         gram_matrix = lax.psum(contract(left_t, left_t, 1, 1), "row")
         left_t = orthonormal(gram_matrix, left_t)
         right_t = lax.psum(contract(left_t, blend, 1, 0), "row")
-        squares = lax.psum(jnp.sum(right_t * right_t, axis=1, keepdims=True), "col")
+        squares = jnp.sum(
+            lax.all_gather(jnp.sum(right_t * right_t, axis=1, keepdims=True), "col"), axis=0
+        )
         factor_t = right_t / (jnp.sqrt(squares) + EPSILON)
     moment = blend - DECAY_LEFT * contract(left_t, right_t, 0, 0)
     accum = contract(left_t, factor_t, 0, 0)

time: 1030 us -> 994 us (0.965)
  blocking collectives: 97.8 us -> 66.9 us
    psum x2 -> x0, blocking collectives: 97.8 us -> none  [local(): squares = lax.psum(jnp.sum(right_t * right_t, axis=1, keepdims=True), 'col')]
    all_gather x0 -> x2, blocking collectives: none -> 66.9 us  [local(): lax.all_gather(jnp.sum(right_t * right_t, axis=1, keepdims=True), 'col')]
where the time goes in v1:
time: 994 us; the launch traced here: 993 us
  waiting for transfers between devices  846 us (85%)
  blocking collectives  66.9 us (7%)
  other arithmetic  48.9 us (5%)
  between operations  14.3 us (1%)
  matrix products  13.5 us (1%)
    psum x2, waiting for transfers between devices, local(): left_t = lax.psum(partial_value, 'col')  399 us
    psum x2, waiting for transfers between devices, local(): right_t = lax.psum(contract(left_t, blend, 1, 0), 'row')  230 us
    psum x2, waiting for transfers between devices, local(): gram_matrix = lax.psum(contract(left_t, left_t, 1, 1), 'row')  217 us
    all_gather x2, blocking collectives, local(): lax.all_gather(jnp.sum(right_t * right_t, axis=1, keepdims=True), 'col')  66.9 us
    another operation x6, other arithmetic, orthonormal(): lower_f = jnp.linalg.cholesky(gram_matrix)  24.8 us
    another operation x4, other arithmetic, orthonormal(): lax.linalg.triangular_solve(lower_f, left_t, left_side=True, lower=True)  21 us
  transfers between devices with their start and end apart: 6, of which 6 were waited for; matrix products, arithmetic and copies ran while one was open for 0% of the time, Pallas kernels for 0%

profile of v1, /device:TPU:1, one launch (start us, length us, event | category | flops | bytes accessed | tf_op | source)
XLA Modules:
  0.0 993.2 jit_solution(5063787613403649436)
XLA Ops:
  8.1 2.7 convolution_bitcast_fusion
  10.9 204.7 %all-reduce.7.cloned.1.call-done = f32[128,256]{0,1:T(8,128)} async-done(((f32[128,256]{0,1:T(8,128)}), f32[128,256]{0,1:T(8,128)}) %all-reduce.7.cloned.1.call-update) | async-done | bytes 131088 | tf_op jit(solution)/shard_map/psum | solution.py:35
  215.6 2.0 fusion.16
  217.7 108.6 %all-reduce.9.cloned.1.call-done = f32[128,128]{0,1:T(8,128)} async-done(((f32[128,128]{0,1:T(8,128)}), f32[128,128]{0,1:T(8,128)}) %all-reduce.9.cloned.1.call-update) | async-done | bytes 65552 | tf_op jit(solution)/shard_map/psum | solution.py:36
  326.3 0.9 copy.11
  328.1 11.7 %cholesky.44 = f32[128,128]{1,0:T(8,128)S(1)} custom-call(f32[128,128]{1,0:T(8,128)S(1)} %fusion.11), custom_call_target="Cholesky" | custom-call | tf_op jit(solution)/shard_map/jit(cholesky)/cholesky | solution.py:25
  341.2 9.8 custom-call.6
  351.3 1.2 fusion.15
  352.6 115.1 %all-reduce.11.cloned.1.call-done = f32[128,448]{0,1:T(8,128)} async-done(((f32[128,448]{0,1:T(8,128)}), f32[128,448]{0,1:T(8,128)}) %all-reduce.11.cloned.1.call-update) | async-done | bytes 229392 | tf_op jit(solution)/shard_map/psum | solution.py:38
  467.7 1.1 multiply_reduce_fusion.1
  468.8 33.4 %all-gather.2 = f32[32,1,128]{2,1,0:T(1,128)S(1)} all-gather(f32[1,1,128]{2,1,0:T(1,128)S(1)} %bitcast.44), channel_id=2, replica_groups=mesh['row'=16,'col'=32] {'col'}, dimensions={0}, use_global_device_ids=true | all-gather | bytes 16896 | tf_op jit(solution)/shard_map/all_gather | solution.py:40
  502.3 1.3 fusion.1
  503.6 194.3 %all-reduce.13.cloned.1.call-done = f32[128,256]{1,0:T(8,128)} async-done(((f32[128,256]{1,0:T(8,128)}), f32[128,256]{1,0:T(8,128)}) %all-reduce.13.cloned.1.call-update) | async-done | bytes 131088 | tf_op jit(solution)/shard_map/psum | solution.py:35
  698.0 1.9 fusion.17
  700.1 108.4 %all-reduce.15.cloned.1.call-done = f32[128,128]{0,1:T(8,128)} async-done(((f32[128,128]{0,1:T(8,128)}), f32[128,128]{0,1:T(8,128)}) %all-reduce.15.cloned.1.call-update) | async-done | bytes 65552 | tf_op jit(solution)/shard_map/psum | solution.py:36
  808.5 1.0 copy.13
  809.6 11.7 %cholesky.55 = f32[128,128]{1,0:T(8,128)S(1)} custom-call(f32[128,128]{1,0:T(8,128)S(1)} %fusion.8), custom_call_target="Cholesky" | custom-call | tf_op jit(solution)/shard_map/jit(cholesky)/cholesky | solution.py:25
  822.6 9.8 custom-call.7
  832.8 1.2 fusion.14
  834.0 115.1 %all-reduce.17.cloned.1.call-done = f32[128,448]{0,1:T(8,128)} async-done(((f32[128,448]{0,1:T(8,128)}), f32[128,448]{0,1:T(8,128)}) %all-reduce.17.cloned.1.call-update) | async-done | bytes 229392 | tf_op jit(solution)/shard_map/psum | solution.py:38
  949.2 1.1 multiply_reduce_fusion
  950.2 33.4 %all-gather.3 = f32[32,1,128]{2,1,0:T(1,128)S(1)} all-gather(f32[1,1,128]{2,1,0:T(1,128)S(1)} %bitcast.45), channel_id=3, replica_groups=mesh['row'=16,'col'=32] {'col'}, dimensions={0}, use_global_device_ids=true | all-gather | bytes 16896 | tf_op jit(solution)/shard_map/all_gather | solution.py:40
  983.8 1.3 convolution_multiply_fusion
  985.1 1.3 fusion
  (45 shorter events, 5.8 us)
Async XLA Ops:
  7.2 0.9 copy-start
  7.2 208.4 %all-reduce.7.cloned.1.call-start = ((), (), s32[]{:S(2)}) async-start(), calls=%async_computation | async-start | bytes 262144 | tf_op jit(solution)/shard_map/psum | solution.py:35
  10.9 315.4 %all-reduce.9.cloned.1.call-start = ((), (), s32[]{:S(2)}) async-start(), calls=%async_computation.1 | async-start | bytes 131072 | tf_op jit(solution)/shard_map/psum | solution.py:36
  217.6 133.7 %copy-start.1 = (f32[256,448]{0,1:T(8,128)S(1)}, f32[256,448]{0,1:T(8,128)}, u32[]{:S(2)}) copy-start(f32[256,448]{0,1:T(8,128)} %param.6) | copy-start | bytes 1376260
  217.6 250.1 %all-reduce.11.cloned.1.call-start = ((), (), s32[]{:S(2)}) async-start(), calls=%async_computation.2 | async-start | bytes 458752 | tf_op jit(solution)/shard_map/psum | solution.py:38
  328.1 22.9 %copy-start.4 = (f32[128,256]{0,1:T(8,128)S(1)}, f32[128,256]{0,1:T(8,128)}, u32[]{:S(2)}) copy-start(f32[128,256]{0,1:T(8,128)} %all-reduce.7.cloned.1.call-done) | copy-start | bytes 393220
  340.5 10.9 %copy-start.2 = (bf16[1,256,448]{1,2,0:T(8,128)(2,1)S(1)}, bf16[1,256,448]{1,2,0:T(8,128)(2,1)}, u32[]{:S(2)}) copy-start(bf16[1,256,448]{1,2,0:T(8,128)(2,1)} %param.7) | copy-start | bytes 688132
  352.6 345.4 %all-reduce.13.cloned.1.call-start = ((), (), s32[]{:S(2)}) async-start(), calls=%async_computation.3 | async-start | bytes 262144 | tf_op jit(solution)/shard_map/psum | solution.py:35
  467.7 34.6 %copy-start.8 = (f32[128,448]{0,1:T(8,128)S(1)}, f32[128,448]{0,1:T(8,128)}, u32[]{:S(2)}) copy-start(f32[128,448]{0,1:T(8,128)} %all-reduce.11.cloned.1.call-done) | copy-start | bytes 688132
  503.6 304.9 %all-reduce.15.cloned.1.call-start = ((), (), s32[]{:S(2)}) async-start(), calls=%async_computation.4 | async-start | bytes 131072 | tf_op jit(solution)/shard_map/psum | solution.py:36
  699.9 249.3 %all-reduce.17.cloned.1.call-start = ((), (), s32[]{:S(2)}) async-start(), calls=%async_computation.5 | async-start | bytes 458752 | tf_op jit(solution)/shard_map/psum | solution.py:38
  808.5 1.0 copy-start.7
  809.6 22.9 %copy-start.5 = (f32[128,256]{1,0:T(8,128)S(1)}, f32[128,256]{1,0:T(8,128)}, u32[]{:S(2)}) copy-start(f32[128,256]{1,0:T(8,128)} %all-reduce.13.cloned.1.call-done) | copy-start | bytes 393220
  949.1 34.6 %copy-start.3 = (f32[128,448]{0,1:T(8,128)S(1)}, f32[128,448]{0,1:T(8,128)}, u32[]{:S(2)}) copy-start(f32[128,448]{0,1:T(8,128)} %all-reduce.17.cloned.1.call-done) | copy-start | bytes 688132
  983.8 1.3 copy-start.6
Sparse Core Ops, SparseCore 0:
  11.0 204.5 all-reduce.6
  219.3 106.8 all-reduce.8
  352.7 114.9 all-reduce.10
  503.7 194.2 all-reduce.12
  701.6 106.8 all-reduce.14
  834.1 114.9 all-reduce.16
